TPU v7x, 256 devices: a whole 4x4x8 slice. The times are simulated.
256 devices in a mesh: shot: 8 (over y, z_lo), space: 32 (over x, z_hi, core).
Axes of the slice: x: 4, y: 4, z: 8 (z_hi: 4, z_lo: 2; z = z_hi * 2 + z_lo), core: 2. Of those that a mesh axis runs over, the one named last changes fastest.
Arguments:
- wave_prev: float32 [8, 512, 128, 128], P('shot', 'space'), may hold values from -6 to 6
- wave_now: float32 [8, 512, 128, 128], P('shot', 'space'), may hold values from -6 to 6
- velocity: float32 [512, 128, 128], P('space'), may hold values from 0.05 to 0.2
- probe_panel: float32 [4, 512, 128, 128], P(None, 'space', 'shot'), may hold values from -6 to 6
- source_depth: int32 [8], P('shot'), may hold values from 0 to 511
- source_column: int32 [8], P('shot'), may hold values from 0 to 16383
- source_strength: float32 [8], P('shot'), may hold values from 2 to 6
- receiver_wells: int32 [8, 512], P('shot'), may hold values from 0 to 16383
Outputs:
- hessian_action: float32 [4, 512, 128, 128], P(None, 'space', 'shot')
All inputs are finite; a program needn't handle non-finite values.
Results may differ from a plain program's by a relative error of at most 0.0003.
Values sent between devices are 32-bit elements; how exact they have to be, the bound alone decides.
No kernel may reach another device: no remote copies, remote signals or barrier semaphores. Data moves between devices by JAX's collectives and lax.ppermute only.
A program may use at most 128 MiB of HBM per device.

v0:
```python
import jax
import jax.numpy as jnp
from jax import lax
from jax.sharding import PartitionSpec as P

CENTER = -205.0 / 72.0
WEIGHTS = (8.0 / 5.0, -1.0 / 5.0, 8.0 / 315.0, -1.0 / 560.0)


def extended(block, sides, width):
    for axis, dim in sides:
        count = lax.axis_size(axis)
        forward = [(i, i + 1) for i in range(count - 1)]
        backward = [(target, source) for source, target in forward]
        low = lax.ppermute(
            lax.slice_in_dim(block, block.shape[dim] - width, None, axis=dim), axis, forward
        )
        high = lax.ppermute(lax.slice_in_dim(block, 0, width, axis=dim), axis, backward)
        block = jnp.concatenate([low, block, high], axis=dim)
    return block


def laplace(padded):
    count_rows = padded.shape[-3] - 8
    middle = padded[..., 4 : 4 + count_rows, :, :]
    count_x = middle.shape[-2]
    count_y = middle.shape[-1]
    lead_pads = [(0, 0)] * (middle.ndim - 2)
    wide_x = jnp.pad(middle, lead_pads + [(4, 4), (0, 0)])
    wide_y = jnp.pad(middle, lead_pads + [(0, 0), (4, 4)])
    stencil = 3.0 * CENTER * middle
    for offset in range(1, 5):
        weight = WEIGHTS[offset - 1]
        stencil = stencil + weight * (
            padded[..., 4 + offset : 4 + offset + count_rows, :, :]
            + padded[..., 4 - offset : 4 - offset + count_rows, :, :]
        )
        stencil = stencil + weight * (
            wide_x[..., 4 + offset : 4 + offset + count_x, :]
            + wide_x[..., 4 - offset : 4 - offset + count_x, :]
        )
        stencil = stencil + weight * (
            wide_y[..., 4 + offset : 4 + offset + count_y]
            + wide_y[..., 4 - offset : 4 - offset + count_y]
        )
    return stencil


def tally(wells, columns):
    return jnp.zeros((columns,), jnp.float32).at[wells].add(1.0)


def per_device(
    wave_prev,
    wave_now,
    velocity,
    probe_panel,
    source_depth,
    source_column,
    source_strength,
    receiver_wells,
):
    shot_count = wave_now.shape[0]
    count_z = wave_now.shape[1]
    width_x = wave_now.shape[2]
    width_y = wave_now.shape[3]
    probe_count = probe_panel.shape[0]
    columns = width_x * width_y
    probes = lax.all_gather(probe_panel, "shot", axis=2, tiled=True)
    first_row = lax.axis_index("space") * count_z
    column_ids = jnp.arange(columns, dtype=jnp.int32).reshape(width_x, width_y)
    now_wide = extended(wave_now, (("space", 1),), 4)
    born_zero = velocity * laplace(now_wide)
    depth_rows = first_row + jnp.arange(count_z, dtype=jnp.int32)
    hit_depth = depth_rows[None, :] == source_depth[:, None]
    hit_column = column_ids[None, :, :] == source_column[:, None, None]
    marks = (hit_depth[:, :, None, None] & hit_column[:, None, :, :]).astype(jnp.float32)
    upcoming = 2.0 * wave_now - wave_prev + born_zero + marks * source_strength[:, None, None, None]
    next_wide = extended(upcoming, (("space", 1),), 4)
    born_one = velocity * laplace(next_wide)
    first_field = probes[:, None] * born_zero[None]
    flat_first = first_field.reshape(probe_count * shot_count, count_z, width_x, width_y)
    first_wide = extended(flat_first, (("space", 1),), 4)
    first_wide = first_wide.reshape(probe_count, shot_count, count_z + 8, width_x, width_y)
    second_field = (
        2.0 * first_field + velocity * laplace(first_wide) + probes[:, None] * born_one[None]
    )
    counts = jax.vmap(lambda wells: tally(wells, columns))(receiver_wells)
    counts = counts.reshape(shot_count, width_x, width_y)[None, :, None]
    late_field = counts * second_field
    weighted = velocity * late_field
    flat_weighted = weighted.reshape(probe_count * shot_count, count_z, width_x, width_y)
    weighted_wide = extended(flat_weighted, (("space", 1),), 4)
    weighted_wide = weighted_wide.reshape(probe_count, shot_count, count_z + 8, width_x, width_y)
    early_field = counts * first_field + 2.0 * late_field + laplace(weighted_wide)
    local_sum = jnp.sum(born_zero[None] * early_field + born_one[None] * late_field, axis=1)
    summed = lax.psum(local_sum, "shot")
    share_rows = width_x // lax.axis_size("shot")
    summed = lax.dynamic_slice_in_dim(summed, lax.axis_index("shot") * share_rows, share_rows, 2)
    return summed / (shot_count * lax.axis_size("shot"))


def solution(mesh):
    return jax.shard_map(
        per_device,
        mesh=mesh,
        in_specs=(
            P("shot", "space", None, None),
            P("shot", "space", None, None),
            P("space", None, None),
            P(None, "space", "shot", None),
            P("shot"),
            P("shot"),
            P("shot"),
            P("shot", None),
        ),
        out_specs=P(None, "space", "shot", None),
        check_vma=False,
    )
```

profile of v0, /device:TPU:1, one launch (start us, length us, event | category | flops | bytes accessed | tf_op | source)
XLA Modules:
  0.0 496.8 jit_solution(8615643306405731458)
XLA Ops:
  7.3 1.1 fusion.131
  8.4 5.1 %collective-permute-start = (f32[1,4,128,128]{3,2,1,0:T(8,128)S(1)}, f32[1,4,128,128]{3,2,1,0:T(8,128)S(1)}, u32[]{:S(2)}, u32[]{:S(2)}) collective-permute-start(f32[1,4,128,128]{3,2,1,0:T(8,128)S(1)} %get-tuple-element.15), channel_id=1, source_target_pairs={{1,0},{2,1},{3,2},{4,3},{5,4},{6,5},{7,6},{8,7},{9,8},{10,9},{11,1... | collective-permute-start | bytes 786440 | tf_op jit(solution)/shard_map/ppermute | solution.py:18
  13.5 3.1 collective-permute-start.1
  20.0 1.5 constant_dynamic-update-slice_fusion.1
  21.6 3.7 select_add_fusion
  25.3 80.6 %all-gather.2.cloned.1.call-done = f32[4,16,128,128]{3,2,1,0:T(8,128)} async-done(((f32[4,16,16,128]{3,2,1,0:T(8,128)}), f32[4,16,128,128]{3,2,1,0:T(8,128)}) %all-gather.2.cloned.1.call-update) | async-done | bytes 4194320 | tf_op jit(solution)/shard_map/all_gather | solution.py:69
  105.9 2.6 broadcast_multiply_fusion
  108.5 1.9 copy-done.3
  110.4 1.6 fusion.129
  112.0 5.2 %collective-permute-start.2 = (f32[4,4,128,128]{3,2,1,0:T(8,128)}, f32[4,4,128,128]{3,2,1,0:T(8,128)}, u32[]{:S(2)}, u32[]{:S(2)}) collective-permute-start(f32[4,4,128,128]{3,2,1,0:T(8,128)} %get-tuple-element.11), channel_id=1, source_target_pairs={{0,1},{1,2},{2,3},{3,4},{4,5},{5,6},{6,7},{7,8},{8,9},{9,10},{10,1... | collective-permute-start | bytes 3145736 | tf_op jit(solution)/shard_map/ppermute | solution.py:15
  117.2 1.9 collective-permute-start.3
  119.2 0.8 fusion.130
  120.0 1.9 collective-permute-start.4
  121.9 4.5 collective-permute-start.5
  126.5 3.3 scatter_custom_fusion
  129.8 21.5 %collective-permute-done.4 = f32[1,4,128,128]{3,2,1,0:T(8,128)S(1)} collective-permute-done((f32[1,4,128,128]{3,2,1,0:T(8,128)}, f32[1,4,128,128]{3,2,1,0:T(8,128)S(1)}, u32[]{:S(2)}, u32[]{:S(2)}) %collective-permute-start.4) | collective-permute-done | bytes 262176 | tf_op jit(solution)/shard_map/ppermute | solution.py:18
  151.3 15.7 %fusion.66 = f32[16,128,128]{2,1,0:T(8,128)S(1)} fusion(f32[1,16,128,128]{3,2,1,0:T(8,128)} %get-tuple-element.7, f32[1,4,128,128]{3,2,1,0:T(8,128)} %collective-permute-done.5, f32[1,4,128,128]{3,2,1,0:T(8,128)S(1)} %collective-permute-done.4, f32[16,128,128]{2,1,0:T(8,128)S(1)} %copy-done.4), kind=kLoop, calls=%fused_computation.126 | loop fusion | flops 12058624 | bytes 3670016 | tf_op jit(solution)/shard_map/mul | solution.py:86
  167.0 3.2 maximum_bitcast_fusion
  170.3 2.6 copy-done.1
  172.9 2.2 slice.454
  175.1 42.2 %multiply_bitcast_fusion = (f32[4,16,128,128]{3,2,1,0:T(8,128)}, f32[4,1,16,128,128]{4,3,2,0,1:T(8,128)}) fusion(f32[16,128,128]{2,1,0:T(8,128)S(1)} %copy-done.4, f32[4,16,128,128]{3,2,1,0:T(8,128)} %all-gather.2.cloned.1.call-done, f32[16,128,128]{2,1,0:T(8,128)S(1)} %fusion.66, f32[4,1,24,128,128]{4,3,2,0,1:T(8,128)} %copy-done.1, ...), kind=kLoop, calls=%fused_computation.99 | loop fusion | flops 47185920 | bytes 53542912 | tf_op jit(solution)/shard_map/reshape | solution.py:92
  217.4 1.8 fusion.128
  219.2 2.1 collective-permute-start.6
  221.3 2.6 collective-permute-start.7
  223.9 13.0 %collective-permute-done.6 = f32[4,4,128,128]{3,2,1,0:T(8,128)S(1)} collective-permute-done((f32[4,4,128,128]{3,2,1,0:T(8,128)S(1)}, f32[4,4,128,128]{3,2,1,0:T(8,128)S(1)}, u32[]{:S(2)}, u32[]{:S(2)}) %collective-permute-start.6) | collective-permute-done | bytes 1048608 | tf_op jit(solution)/shard_map/ppermute | solution.py:15
  237.0 10.9 %collective-permute-done.7 = f32[4,4,128,128]{3,2,1,0:T(8,128)S(1)} collective-permute-done((f32[4,4,128,128]{3,2,1,0:T(8,128)S(1)}, f32[4,4,128,128]{3,2,1,0:T(8,128)S(1)}, u32[]{:S(2)}, u32[]{:S(2)}) %collective-permute-start.7) | collective-permute-done | bytes 1048608 | tf_op jit(solution)/shard_map/ppermute | solution.py:18
  247.8 0.8 maximum_bitcast_fusion.1
  248.6 2.5 slice.479
  251.1 1.6 copy-done
  252.7 46.0 %fusion.55 = f32[4,16,128,128]{3,2,1,0:T(8,128)} fusion(f32[4,1,16,128,128]{4,3,2,0,1:T(8,128)} %get-tuple-element.6, f32[4,1,16,128,128]{4,3,2,0,1:T(8,128)} %slice.479, f32[4,1,24,128,128]{4,3,2,0,1:T(8,128)} %copy-done, f32[16,128,128]{2,1,0:T(8,128)S(1)} %fusion.66, f32[128,128]{1,0:T(8,128)S(1)} %bitcast.47, f32[16,128,128]{2,1,0:T(8,128)S(1)} %bitcast.45, ...), kind=kLoop, calls=%fused_computation.102 | loop fusion | flops 47185920 | bytes 53542912 | tf_op jit(solution)/shard_map/reduce_sum | solution.py:96
  298.8 189.2 %all-reduce.10.cloned.1.call-done = f32[4,16,128,128]{3,2,1,0:T(8,128)} async-done(((f32[4,16,128,128]{3,2,1,0:T(8,128)}), f32[4,16,128,128]{3,2,1,0:T(8,128)}) %all-reduce.10.cloned.1.call-update) | async-done | bytes 4194320 | tf_op jit(solution)/shard_map/psum | solution.py:97
  488.0 1.9 dynamic-slice_multiply_fusion
  (30 shorter events, 2.2 us)
Async XLA Ops:
  6.5 15.0 %copy-start.5 = (f32[1,16,128,128]{3,2,1,0:T(8,128)S(1)}, f32[1,16,128,128]{3,2,1,0:T(8,128)}, u32[]{:S(2)}) copy-start(f32[1,16,128,128]{3,2,1,0:T(8,128)} %param.9) | copy-start | bytes 3145732
  6.5 15.0 %copy-start.4 = (f32[16,128,128]{2,1,0:T(8,128)S(1)}, f32[16,128,128]{2,1,0:T(8,128)}, u32[]{:S(2)}) copy-start(f32[16,128,128]{2,1,0:T(8,128)} %param.10) | copy-start | bytes 3145732
  6.5 99.3 %all-gather.2.cloned.1.call-start = ((), (), s32[]{:S(2)}) async-start(), calls=%async_computation | async-start | bytes 4718592 | tf_op jit(solution)/shard_map/all_gather | solution.py:69
  7.3 480.8 %all-reduce.10.cloned.1.call-start = ((), (), s32[]{:S(2)}) async-start(), calls=%async_computation.1 | async-start | bytes 8388608 | tf_op jit(solution)/shard_map/psum | solution.py:97
  8.4 13.1 %collective-permute-start = (f32[1,4,128,128]{3,2,1,0:T(8,128)S(1)}, f32[1,4,128,128]{3,2,1,0:T(8,128)S(1)}, u32[]{:S(2)}, u32[]{:S(2)}) collective-permute-start(f32[1,4,128,128]{3,2,1,0:T(8,128)S(1)} %get-tuple-element.15), channel_id=1, source_target_pairs={{1,0},{2,1},{3,2},{4,3},{5,4},{6,5},{7,6},{8,7},{9,8},{10,9},{11,1... | collective-permute-start | bytes 786440 | tf_op jit(solution)/shard_map/ppermute | solution.py:18
  13.5 6.4 %collective-permute-start.1 = (f32[1,4,128,128]{3,2,1,0:T(8,128)S(1)}, f32[1,4,128,128]{3,2,1,0:T(8,128)S(1)}, u32[]{:S(2)}, u32[]{:S(2)}) collective-permute-start(f32[1,4,128,128]{3,2,1,0:T(8,128)S(1)} %get-tuple-element.16), channel_id=1, source_target_pairs={{0,1},{1,2},{2,3},{3,4},{4,5},{5,6},{6,7},{7,8},{8,9},{9,10},{10,1... | collective-permute-start | bytes 786440 | tf_op jit(solution)/shard_map/ppermute | solution.py:15
  17.9 3.7 copy-start.7
  108.5 1.9 copy-start.3
  110.4 8.7 %copy-start.6 = (f32[1,16,128,128]{3,2,1,0:T(8,128)S(1)}, f32[1,16,128,128]{3,2,1,0:T(8,128)}, u32[]{:S(2)}) copy-start(f32[1,16,128,128]{3,2,1,0:T(8,128)} %get-tuple-element.7) | copy-start | bytes 3145732
  112.0 55.0 %collective-permute-start.2 = (f32[4,4,128,128]{3,2,1,0:T(8,128)}, f32[4,4,128,128]{3,2,1,0:T(8,128)}, u32[]{:S(2)}, u32[]{:S(2)}) collective-permute-start(f32[4,4,128,128]{3,2,1,0:T(8,128)} %get-tuple-element.11), channel_id=1, source_target_pairs={{0,1},{1,2},{2,3},{3,4},{4,5},{5,6},{6,7},{7,8},{8,9},{9,10},{10,1... | collective-permute-start | bytes 3145736 | tf_op jit(solution)/shard_map/ppermute | solution.py:15
  117.2 49.8 %collective-permute-start.3 = (f32[4,4,128,128]{3,2,1,0:T(8,128)}, f32[4,4,128,128]{3,2,1,0:T(8,128)}, u32[]{:S(2)}, u32[]{:S(2)}) collective-permute-start(f32[4,4,128,128]{3,2,1,0:T(8,128)} %get-tuple-element.12), channel_id=1, source_target_pairs={{1,0},{2,1},{3,2},{4,3},{5,4},{6,5},{7,6},{8,7},{9,8},{10,9},{11,1... | collective-permute-start | bytes 3145736 | tf_op jit(solution)/shard_map/ppermute | solution.py:18
  120.0 31.3 %collective-permute-start.4 = (f32[1,4,128,128]{3,2,1,0:T(8,128)}, f32[1,4,128,128]{3,2,1,0:T(8,128)S(1)}, u32[]{:S(2)}, u32[]{:S(2)}) collective-permute-start(f32[1,4,128,128]{3,2,1,0:T(8,128)} %get-tuple-element.13), channel_id=1, source_target_pairs={{1,0},{2,1},{3,2},{4,3},{5,4},{6,5},{7,6},{8,7},{9,8},{10,9},{11,1... | collective-permute-start | bytes 786440 | tf_op jit(solution)/shard_map/ppermute | solution.py:18
  121.9 29.4 %collective-permute-start.5 = (f32[1,4,128,128]{3,2,1,0:T(8,128)}, f32[1,4,128,128]{3,2,1,0:T(8,128)}, u32[]{:S(2)}, u32[]{:S(2)}) collective-permute-start(f32[1,4,128,128]{3,2,1,0:T(8,128)} %get-tuple-element.14), channel_id=1, source_target_pairs={{0,1},{1,2},{2,3},{3,4},{4,5},{5,6},{6,7},{7,8},{8,9},{9,10},{10,1... | collective-permute-start | bytes 786440 | tf_op jit(solution)/shard_map/ppermute | solution.py:15
  170.3 2.7 copy-start.1
  217.4 30.5 %copy-start.2 = (f32[4,16,128,128]{3,2,1,0:T(8,128)S(1)}, f32[4,16,128,128]{3,2,1,0:T(8,128)}, u32[]{:S(2)}) copy-start(f32[4,16,128,128]{3,2,1,0:T(8,128)} %get-tuple-element.5) | copy-start | bytes 12582916
  219.2 17.7 %collective-permute-start.6 = (f32[4,4,128,128]{3,2,1,0:T(8,128)S(1)}, f32[4,4,128,128]{3,2,1,0:T(8,128)S(1)}, u32[]{:S(2)}, u32[]{:S(2)}) collective-permute-start(f32[4,4,128,128]{3,2,1,0:T(8,128)S(1)} %get-tuple-element.9), channel_id=1, source_target_pairs={{0,1},{1,2},{2,3},{3,4},{4,5},{5,6},{6,7},{7,8},{8,9},{9,10},{10,1... | collective-permute-start | bytes 3145736 | tf_op jit(solution)/shard_map/ppermute | solution.py:15
  221.3 26.5 %collective-permute-start.7 = (f32[4,4,128,128]{3,2,1,0:T(8,128)S(1)}, f32[4,4,128,128]{3,2,1,0:T(8,128)S(1)}, u32[]{:S(2)}, u32[]{:S(2)}) collective-permute-start(f32[4,4,128,128]{3,2,1,0:T(8,128)S(1)} %get-tuple-element.10), channel_id=1, source_target_pairs={{1,0},{2,1},{3,2},{4,3},{5,4},{6,5},{7,6},{8,7},{9,8},{10,9},{11,1... | collective-permute-start | bytes 3145736 | tf_op jit(solution)/shard_map/ppermute | solution.py:18
  248.6 4.1 copy-start
Sparse Core Ops, SparseCore 0:
  9.1 96.7 all-gather.1
  298.9 189.0 all-reduce.9
where the time goes:
time: 497 us
  waiting for transfers between devices  317 us (64%)
  other arithmetic  120 us (24%)
  starting transfers between devices  26.5 us (5%)
  local copies, waits for them, and re-layouts  17.7 us (4%)
  between operations  15.7 us (3%)
    psum x1, waiting for transfers between devices, per_device(): summed = lax.psum(local_sum, 'shot')  189 us
    all_gather x1, waiting for transfers between devices, per_device(): probes = lax.all_gather(probe_panel, 'shot', axis=2, tiled=True)  80.6 us
    reduce_sum x1, other arithmetic, per_device(): jnp.sum(born_zero[None] * early_field + born_one[None] * late_field, axis=1)  46 us
    reshape x1, other arithmetic, per_device(): weighted.reshape(probe_count * shot_count, count_z, width_x, width_y)  42.2 us
    ppermute x4, waiting for transfers between devices, extended(): lax.ppermute(lax.slice_in_dim(block, 0, width, axis=dim), axis, backward)  32.5 us
    mul x1, other arithmetic, per_device(): probes[:, None] * born_one[None]  15.7 us
    ppermute x4, starting transfers between devices, extended(): lax.ppermute(lax.slice_in_dim(block, block.shape[dim] - width, None, axis...  14.9 us
    ppermute x4, waiting for transfers between devices, extended(): lax.ppermute(lax.slice_in_dim(block, block.shape[dim] - width, None, axis...  13.6 us
  transfers between devices with their start and end apart: 10, of which 6 were waited for; matrix products, arithmetic and copies ran while one was open for 5% of the time, Pallas kernels for 0%

commit v1 on v0

--- a/solution.py
+++ b/solution.py
@@ -94,7 +94,7 @@
     weighted_wide = weighted_wide.reshape(probe_count, shot_count, count_z + 8, width_x, width_y)
     early_field = counts * first_field + 2.0 * late_field + laplace(weighted_wide)
     local_sum = jnp.sum(born_zero[None] * early_field + born_one[None] * late_field, axis=1)
-    summed = lax.psum(local_sum, "shot")
+    summed = jnp.sum(lax.all_gather(local_sum, "shot"), axis=0)
     share_rows = width_x // lax.axis_size("shot")
     summed = lax.dynamic_slice_in_dim(summed, lax.axis_index("shot") * share_rows, share_rows, 2)
     return summed / (shot_count * lax.axis_size("shot"))

time: 497 us -> 960 us (1.93)
  waiting for transfers between devices: 317 us -> 772 us
    all_gather x0 -> x1, waiting for transfers between devices: none -> 644 us  [per_device(): summed = jnp.sum(lax.all_gather(local_sum, 'shot'), axis=0)]
    psum x1 -> x0, waiting for transfers between devices: 189 us -> none  [per_device(): summed = lax.psum(local_sum, 'shot')]
    add x0 -> x1, other arithmetic: none -> 43 us  [per_device(): born_zero[None] * early_field + born_one[None] * late_field]
    reduce_sum x1, other arithmetic: 46 us -> 12.2 us  [per_device(): summed = jnp.sum(lax.all_gather(local_sum, 'shot'), axis=0)]
  transfers between devices with their start and end apart: 10 -> 10, of which waited for: 6 -> 6; matrix products, arithmetic and copies ran while one was open for 5% -> 3% of each run, Pallas kernels for 0% -> 0%
where the time goes in v1:
time: 960 us
  waiting for transfers between devices  772 us (80%)
  other arithmetic  128 us (13%)
  starting transfers between devices  26.5 us (3%)
  local copies, waits for them, and re-layouts  17.6 us (2%)
  between operations  15.7 us (2%)
    all_gather x1, waiting for transfers between devices, per_device(): summed = jnp.sum(lax.all_gather(local_sum, 'shot'), axis=0)  644 us
    all_gather x1, waiting for transfers between devices, per_device(): probes = lax.all_gather(probe_panel, 'shot', axis=2, tiled=True)  80.6 us
    add x1, other arithmetic, per_device(): born_zero[None] * early_field + born_one[None] * late_field  43 us
    reshape x1, other arithmetic, per_device(): weighted.reshape(probe_count * shot_count, count_z, width_x, width_y)  42.2 us
    ppermute x4, waiting for transfers between devices, extended(): lax.ppermute(lax.slice_in_dim(block, 0, width, axis=dim), axis, backward)  32.5 us
  transfers between devices with their start and end apart: 10, of which 6 were waited for; matrix products, arithmetic and copies ran while one was open for 3% of the time, Pallas kernels for 0%

profile of v1, /device:TPU:1, one launch (start us, length us, event | category | flops | bytes accessed | tf_op | source)
XLA Modules:
  0.0 959.8 jit_solution(5243197905707910539)
XLA Ops:
  7.3 1.1 fusion.129
  8.4 5.1 collective-permute-start
  13.5 3.1 collective-permute-start.1
  20.0 1.5 constant_dynamic-update-slice_fusion.1
  21.6 3.7 select_add_fusion
  25.3 80.6 %all-gather.4.cloned.1.call-done = f32[4,16,128,128]{3,2,1,0:T(8,128)} async-done(((f32[4,16,16,128]{3,2,1,0:T(8,128)}), f32[4,16,128,128]{3,2,1,0:T(8,128)}) %all-gather.4.cloned.1.call-update) | async-done | bytes 4194320 | tf_op jit(solution)/shard_map/all_gather | solution.py:69
  105.9 2.6 broadcast_multiply_fusion
  108.5 1.9 copy-done.3
  110.4 1.6 fusion.127
  112.0 5.2 collective-permute-start.2
  117.2 1.9 collective-permute-start.3
  119.2 0.8 fusion.128
  120.0 1.9 collective-permute-start.4
  121.9 4.5 collective-permute-start.5
  126.5 3.3 scatter_custom_fusion
  129.8 21.5 %collective-permute-done.4 = f32[1,4,128,128]{3,2,1,0:T(8,128)S(1)} collective-permute-done((f32[1,4,128,128]{3,2,1,0:T(8,128)}, f32[1,4,128,128]{3,2,1,0:T(8,128)S(1)}, u32[]{:S(2)}, u32[]{:S(2)}) %collective-permute-start.4) | collective-permute-done | bytes 262176 | tf_op jit(solution)/shard_map/ppermute | solution.py:18
  151.3 15.7 %fusion.65 = f32[16,128,128]{2,1,0:T(8,128)S(1)} fusion(f32[1,16,128,128]{3,2,1,0:T(8,128)} %get-tuple-element.7, f32[1,4,128,128]{3,2,1,0:T(8,128)} %collective-permute-done.5, f32[1,4,128,128]{3,2,1,0:T(8,128)S(1)} %collective-permute-done.4, f32[16,128,128]{2,1,0:T(8,128)S(1)} %copy-done.4), kind=kLoop, calls=%fused_computation.128 | loop fusion | flops 12058624 | bytes 3670016 | tf_op jit(solution)/shard_map/mul | solution.py:86
  167.0 3.2 maximum_bitcast_fusion
  170.3 2.6 copy-done.1
  172.9 2.2 slice.454
  175.1 42.2 %fusion.53 = (f32[4,16,128,128]{3,2,1,0:T(8,128)}, f32[4,1,16,128,128]{4,3,2,1,0:T(8,128)}) fusion(f32[16,128,128]{2,1,0:T(8,128)S(1)} %copy-done.4, f32[4,16,128,128]{3,2,1,0:T(8,128)} %all-gather.4.cloned.1.call-done, f32[16,128,128]{2,1,0:T(8,128)S(1)} %fusion.65, f32[4,1,24,128,128]{4,3,2,0,1:T(8,128)} %copy-done.1, f32[4,1,16,128,128]{4,3,2,0,1:T(8,128)} %slice.454, ...), kind=kLoop, calls=%fused_computation.99 | loop fusion | flops 47185920 | bytes 53542912 | tf_op jit(solution)/shard_map/reshape | solution.py:92
  217.4 1.8 fusion.126
  219.2 2.1 collective-permute-start.6
  221.3 2.6 collective-permute-start.7
  223.9 13.0 %collective-permute-done.6 = f32[4,4,128,128]{3,2,1,0:T(8,128)S(1)} collective-permute-done((f32[4,4,128,128]{3,2,1,0:T(8,128)S(1)}, f32[4,4,128,128]{3,2,1,0:T(8,128)S(1)}, u32[]{:S(2)}, u32[]{:S(2)}) %collective-permute-start.6) | collective-permute-done | bytes 1048608 | tf_op jit(solution)/shard_map/ppermute | solution.py:15
  237.0 10.9 %collective-permute-done.7 = f32[4,4,128,128]{3,2,1,0:T(8,128)S(1)} collective-permute-done((f32[4,4,128,128]{3,2,1,0:T(8,128)S(1)}, f32[4,4,128,128]{3,2,1,0:T(8,128)S(1)}, u32[]{:S(2)}, u32[]{:S(2)}) %collective-permute-start.7) | collective-permute-done | bytes 1048608 | tf_op jit(solution)/shard_map/ppermute | solution.py:18
  248.6 2.4 slice.479
  251.0 1.5 copy-done
  252.5 43.0 %bitcast_add_fusion = f32[4,1,16,128,128]{4,3,2,1,0:T(8,128)} fusion(f32[4,1,16,128,128]{4,3,2,1,0:T(8,128)} %get-tuple-element.6, f32[4,1,16,128,128]{4,3,2,0,1:T(8,128)} %slice.479, f32[4,1,24,128,128]{4,3,2,0,1:T(8,128)} %copy-done, f32[16,128,128]{2,1,0:T(8,128)S(1)} %fusion.65, f32[128,128]{1,0:T(8,128)S(1)} %bitcast.64, ...), kind=kLoop, calls=%fused_computation.97 | loop fusion | flops 47185920 | bytes 53542912 | tf_op jit(solution)/shard_map/add | solution.py:96
  295.6 644.3 %all-gather.6.cloned.1.call-done = f32[32,1,16,128,128]{4,3,2,1,0:T(8,128)} async-done(((f32[4,1,16,128,128]{4,3,2,1,0:T(8,128)}), f32[32,1,16,128,128]{4,3,2,1,0:T(8,128)}) %all-gather.6.cloned.1.call-update) | async-done | bytes 33554448 | tf_op jit(solution)/shard_map/all_gather | solution.py:97
  939.9 12.2 %bitcast_reduce_fusion = f32[4,16,128,128]{3,2,1,0:T(8,128)S(1)} fusion(f32[8,4,16,128,128]{4,3,2,1,0:T(8,128)} %bitcast.59), kind=kLoop, calls=%fused_computation.1 | loop fusion | flops 7340032 | bytes 37748736 | tf_op jit(solution)/shard_map/reduce_sum | solution.py:97
  952.1 0.9 dynamic-slice_multiply_fusion
  (31 shorter events, 3.0 us)
Async XLA Ops:
  6.5 15.0 %copy-start.5 = (f32[1,16,128,128]{3,2,1,0:T(8,128)S(1)}, f32[1,16,128,128]{3,2,1,0:T(8,128)}, u32[]{:S(2)}) copy-start(f32[1,16,128,128]{3,2,1,0:T(8,128)} %param.9) | copy-start | bytes 3145732
  6.5 15.0 %copy-start.4 = (f32[16,128,128]{2,1,0:T(8,128)S(1)}, f32[16,128,128]{2,1,0:T(8,128)}, u32[]{:S(2)}) copy-start(f32[16,128,128]{2,1,0:T(8,128)} %param.10) | copy-start | bytes 3145732
  6.5 99.3 %all-gather.4.cloned.1.call-start = ((), (), s32[]{:S(2)}) async-start(), calls=%async_computation | async-start | bytes 4718592 | tf_op jit(solution)/shard_map/all_gather | solution.py:69
  7.3 932.7 %all-gather.6.cloned.1.call-start = ((), (), s32[]{:S(2)}) async-start(), calls=%async_computation.1 | async-start | bytes 37748736 | tf_op jit(solution)/shard_map/all_gather | solution.py:97
  8.4 13.1 %collective-permute-start = (f32[1,4,128,128]{3,2,1,0:T(8,128)S(1)}, f32[1,4,128,128]{3,2,1,0:T(8,128)S(1)}, u32[]{:S(2)}, u32[]{:S(2)}) collective-permute-start(f32[1,4,128,128]{3,2,1,0:T(8,128)S(1)} %get-tuple-element.15), channel_id=1, source_target_pairs={{1,0},{2,1},{3,2},{4,3},{5,4},{6,5},{7,6},{8,7},{9,8},{10,9},{11,1... | collective-permute-start | bytes 786440 | tf_op jit(solution)/shard_map/ppermute | solution.py:18
  13.5 6.4 collective-permute-start.1
  17.9 3.7 copy-start.7
  108.5 1.9 copy-start.3
  110.4 8.7 copy-start.6
  112.0 55.0 %collective-permute-start.2 = (f32[4,4,128,128]{3,2,1,0:T(8,128)}, f32[4,4,128,128]{3,2,1,0:T(8,128)}, u32[]{:S(2)}, u32[]{:S(2)}) collective-permute-start(f32[4,4,128,128]{3,2,1,0:T(8,128)} %get-tuple-element.11), channel_id=1, source_target_pairs={{0,1},{1,2},{2,3},{3,4},{4,5},{5,6},{6,7},{7,8},{8,9},{9,10},{10,1... | collective-permute-start | bytes 3145736 | tf_op jit(solution)/shard_map/ppermute | solution.py:15
  117.2 49.8 %collective-permute-start.3 = (f32[4,4,128,128]{3,2,1,0:T(8,128)}, f32[4,4,128,128]{3,2,1,0:T(8,128)}, u32[]{:S(2)}, u32[]{:S(2)}) collective-permute-start(f32[4,4,128,128]{3,2,1,0:T(8,128)} %get-tuple-element.12), channel_id=1, source_target_pairs={{1,0},{2,1},{3,2},{4,3},{5,4},{6,5},{7,6},{8,7},{9,8},{10,9},{11,1... | collective-permute-start | bytes 3145736 | tf_op jit(solution)/shard_map/ppermute | solution.py:18
  120.0 31.3 %collective-permute-start.4 = (f32[1,4,128,128]{3,2,1,0:T(8,128)}, f32[1,4,128,128]{3,2,1,0:T(8,128)S(1)}, u32[]{:S(2)}, u32[]{:S(2)}) collective-permute-start(f32[1,4,128,128]{3,2,1,0:T(8,128)} %get-tuple-element.13), channel_id=1, source_target_pairs={{1,0},{2,1},{3,2},{4,3},{5,4},{6,5},{7,6},{8,7},{9,8},{10,9},{11,1... | collective-permute-start | bytes 786440 | tf_op jit(solution)/shard_map/ppermute | solution.py:18
  121.9 29.4 %collective-permute-start.5 = (f32[1,4,128,128]{3,2,1,0:T(8,128)}, f32[1,4,128,128]{3,2,1,0:T(8,128)}, u32[]{:S(2)}, u32[]{:S(2)}) collective-permute-start(f32[1,4,128,128]{3,2,1,0:T(8,128)} %get-tuple-element.14), channel_id=1, source_target_pairs={{0,1},{1,2},{2,3},{3,4},{4,5},{5,6},{6,7},{7,8},{8,9},{9,10},{10,1... | collective-permute-start | bytes 786440 | tf_op jit(solution)/shard_map/ppermute | solution.py:15
  170.3 2.7 copy-start.1
  217.4 30.5 %copy-start.2 = (f32[4,16,128,128]{3,2,1,0:T(8,128)S(1)}, f32[4,16,128,128]{3,2,1,0:T(8,128)}, u32[]{:S(2)}) copy-start(f32[4,16,128,128]{3,2,1,0:T(8,128)} %get-tuple-element.5) | copy-start | bytes 12582916
  219.2 17.7 %collective-permute-start.6 = (f32[4,4,128,128]{3,2,1,0:T(8,128)S(1)}, f32[4,4,128,128]{3,2,1,0:T(8,128)S(1)}, u32[]{:S(2)}, u32[]{:S(2)}) collective-permute-start(f32[4,4,128,128]{3,2,1,0:T(8,128)S(1)} %get-tuple-element.9), channel_id=1, source_target_pairs={{0,1},{1,2},{2,3},{3,4},{4,5},{5,6},{6,7},{7,8},{8,9},{9,10},{10,1... | collective-permute-start | bytes 3145736 | tf_op jit(solution)/shard_map/ppermute | solution.py:15
  221.3 26.5 %collective-permute-start.7 = (f32[4,4,128,128]{3,2,1,0:T(8,128)S(1)}, f32[4,4,128,128]{3,2,1,0:T(8,128)S(1)}, u32[]{:S(2)}, u32[]{:S(2)}) collective-permute-start(f32[4,4,128,128]{3,2,1,0:T(8,128)S(1)} %get-tuple-element.10), channel_id=1, source_target_pairs={{1,0},{2,1},{3,2},{4,3},{5,4},{6,5},{7,6},{8,7},{9,8},{10,9},{11,1... | collective-permute-start | bytes 3145736 | tf_op jit(solution)/shard_map/ppermute | solution.py:18
  248.6 3.9 copy-start
Sparse Core Ops, SparseCore 0:
  9.1 96.7 all-gather.3
  295.7 644.1 all-gather.5
